TPU v7x, 32 devices: a whole 2x2x4 slice. The times are simulated.
32 devices in a mesh: row: 4 (over z), col: 8 (over y, x, core).
Axes of the slice: x: 2, y: 2, z: 4, core: 2. Of those that a mesh axis runs over, the one named last changes fastest.
Arguments:
- dec_src: float32 [2304, 8192], P('col', 'row'), may hold values from -6 to 6
- enc_tgt: float32 [2304, 16384], P('row', 'col'), may hold values from -0.125 to 0.125
- src_coacts: float32 [512, 8192], P('col', 'row'), may hold values from -6 to 6
- tgt_coacts: float32 [512, 16384], P('row', 'col'), may hold values from -6 to 6
- eval_src: float32 [512, 8192], P('col', 'row'), may hold values from -6 to 6
- enc_bias: float32 [16384], P('col'), may hold values from -0.5 to 0.5
- dec_tgt: float32 [2304, 16384], P('row', 'col'), may hold values from -0.046875 to 0.046875
- tile_mask: int32 [128, 256], P('row', 'col'), may hold values from 0 to 1, as said below
Outputs:
- recon: float32 [512, 2304], P('col', 'row')
Inputs may be any that keep to these rules, and one draw needn't show every extreme that they name: `tile_mask`: 1 keeps a tile, 0 prunes it; the share of kept tiles differs between regions of the grid.
All inputs are finite; a program needn't handle non-finite values.
Results may differ from a plain program's by a relative error of at most 0.0003.
Values sent between devices are 32-bit elements; how exact they have to be, the bound alone decides.
A program may use at most 192 MiB of HBM per device.

v0:
```python
import jax
import jax.numpy as jnp
from jax import lax
from jax.sharding import PartitionSpec as P

S = 8192
TILE = 64
PRECISE = lax.Precision.HIGHEST


def contract_first(left, right):
    return lax.dot_general(
        left, right, (((0,), (0,)), ((), ())), precision=PRECISE, preferred_element_type=jnp.float32
    )


def local(dec_src, enc_tgt, src_coacts, tgt_coacts, eval_src, enc_bias, dec_tgt, tile_mask):
    src_count = dec_src.shape[1]
    tgt_count = enc_tgt.shape[1]
    enc_full = lax.all_gather(enc_tgt, "row", axis=0, tiled=True)
    src_full, eval_full = (
        lax.all_gather(src_coacts, "col", axis=0, tiled=True),
        lax.all_gather(eval_src, "col", axis=0, tiled=True),
    )
    virtual = contract_first(lax.all_gather(dec_src, "col", axis=0, tiled=True), enc_full)
    coact = contract_first(src_full, lax.all_gather(tgt_coacts, "row", axis=0, tiled=True))
    coact = coact * (1.0 / jnp.sqrt(jnp.float32(src_full.shape[0])))
    tile_rows, tile_cols = tile_mask.shape
    mask_float = tile_mask.astype(jnp.float32)
    weighted = (
        (virtual * coact).reshape(tile_rows, TILE, tile_cols, TILE) * mask_float[:, None, :, None]
    ).reshape(src_count, tgt_count)
    partial_pre = jnp.dot(
        eval_full, weighted, precision=PRECISE, preferred_element_type=jnp.float32
    )
    scale = 1.0 / jnp.sqrt(jnp.float32(S))
    pre_acts = lax.psum(partial_pre, "row")
    hidden = jnp.maximum(pre_acts * scale + enc_bias[None, :], 0.0)
    recon_part = lax.dot_general(
        hidden,
        dec_tgt,
        (((1,), (1,)), ((), ())),
        precision=PRECISE,
        preferred_element_type=jnp.float32,
    )
    return lax.psum_scatter(recon_part, "col", scatter_dimension=0, tiled=True)


def solution(mesh):
    return jax.shard_map(
        local,
        mesh=mesh,
        in_specs=(
            P("col", "row"),
            P("row", "col"),
            P("col", "row"),
            P("row", "col"),
            P("col", "row"),
            P("col"),
            P("row", "col"),
            P("row", "col"),
        ),
        out_specs=P("col", "row"),
        check_vma=False,
    )
```

profile of v0, /device:TPU:0, one launch (start us, length us, event | category | flops | bytes accessed | tf_op | source)
XLA Modules:
  0.0 963.4 jit_solution(13110801990855593298)
XLA Ops:
  6.5 0.7 all-gather.12.cloned.1.call-update
  7.3 0.0 all-gather.10.cloned.1.call-start
  7.3 0.7 all-gather.10.cloned.1.call-update
  8.0 0.0 all-gather.8.cloned.1.call-start
  8.1 0.7 all-gather.8.cloned.1.call-update
  8.7 0.0 all-gather.6.cloned.1.call-start
  8.8 0.5 all-gather.6.cloned.1.call-update
  9.3 0.0 all-gather.14.cloned.1.call-start
  9.4 0.5 all-gather.14.cloned.1.call-update
  9.9 0.0 all-reduce.2.cloned.1.call-start
  10.0 11.9 %mul.29 = f32[32,64,32,64]{3,2,1,0:T(8,128)} broadcast(f32[32,32]{1,0:T(8,128)S(1)} %convert_element_type.3), dimensions={0,2} | broadcast | bytes 16781312 | tf_op jit(solution)/shard_map/mul | solution.py:31
  21.9 29.0 %mul.30 = f32[2048,2048]{1,0:T(8,128)} reshape(f32[32,64,32,64]{3,2,1,0:T(8,128)} %mul.29) | data formatting | bytes 33554432 | tf_op jit(solution)/shard_map/mul | solution.py:31
  50.9 41.5 %all-gather.12.cloned.1.call-done = f32[512,2048]{1,0:T(8,128)} async-done(((f32[128,2048]{1,0:T(8,128)}), f32[512,2048]{1,0:T(8,128)}) %all-gather.12.cloned.1.call-update) | async-done | bytes 4194320 | tf_op jit(solution)/shard_map/all_gather | solution.py:26
  92.4 37.0 %all-gather.10.cloned.1.call-done = f32[512,2048]{1,0:T(8,128)} async-done(((f32[64,2048]{1,0:T(8,128)}), f32[512,2048]{1,0:T(8,128)}) %all-gather.10.cloned.1.call-update) | async-done | bytes 4194320 | tf_op jit(solution)/shard_map/all_gather | solution.py:22
  129.4 31.4 %fusion.19 = f32[2048,2048]{1,0:T(8,128)} fusion(f32[512,2048]{1,0:T(8,128)} %all-gather.10.cloned.1.call-done, f32[512,2048]{1,0:T(8,128)} %all-gather.12.cloned.1.call-done), kind=kOutput, calls=%fused_computation.17 | convolution fusion | flops 25769803776 | bytes 25165824 | tf_op jit(solution)/shard_map/dot_general | solution.py:12
  160.8 292.8 %all-gather.8.cloned.1.call-done = f32[2304,2048]{1,0:T(8,128)} async-done(((f32[576,2048]{1,0:T(8,128)}), f32[2304,2048]{1,0:T(8,128)}) %all-gather.8.cloned.1.call-update) | async-done | bytes 18874384 | tf_op jit(solution)/shard_map/all_gather | solution.py:20
  453.6 99.2 %all-gather.6.cloned.1.call-done = f32[2304,2048]{1,0:T(8,128)} async-done(((f32[288,2048]{1,0:T(8,128)}), f32[2304,2048]{1,0:T(8,128)}) %all-gather.6.cloned.1.call-update) | async-done | bytes 18874384 | tf_op jit(solution)/shard_map/all_gather | solution.py:25
  552.8 125.5 %fusion.18 = f32[2048,2048]{1,0:T(8,128)} fusion(f32[2304,2048]{1,0:T(8,128)} %all-gather.6.cloned.1.call-done, f32[2304,2048]{1,0:T(8,128)} %all-gather.8.cloned.1.call-done), kind=kOutput, calls=%fused_computation.16 | convolution fusion | flops 115964116992 | bytes 54525952 | tf_op jit(solution)/shard_map/dot_general | solution.py:12
  678.3 0.0 all-gather.14.cloned.1.call-done
  678.4 62.9 %fusion.9 = f32[512,2048]{0,1:T(8,128)} fusion(f32[512,2048]{1,0:T(8,128)} %all-gather.14.cloned.1.call-done, f32[2048,2048]{1,0:T(8,128)} %mul.30, f32[2048,2048]{1,0:T(8,128)} %fusion.18, f32[2048,2048]{1,0:T(8,128)} %fusion.19), kind=kOutput, calls=%fused_computation.9 | convolution fusion | flops 25782386688 | bytes 58720256 | tf_op jit(solution)/shard_map/dot_general | solution.py:33
  741.3 0.0 reduce-scatter.2.cloned.1.call-start
  741.3 155.1 %all-reduce.2.cloned.1.call-done = f32[512,2048]{0,1:T(8,128)} async-done(((f32[512,2048]{0,1:T(8,128)}), f32[512,2048]{0,1:T(8,128)}) %all-reduce.2.cloned.1.call-update) | async-done | bytes 4194320 | tf_op jit(solution)/shard_map/psum | solution.py:37
  896.4 23.6 %fusion.5 = f32[512,576]{1,0:T(8,128)} fusion(f32[576,2048]{1,0:T(8,128)} %param.14, f32[512,2048]{0,1:T(8,128)} %all-reduce.2.cloned.1.call-done, f32[2048]{0:T(1024)S(1)} %copy-done.1), kind=kOutput, calls=%fused_computation.5 | convolution fusion | flops 7250903040 | bytes 10100736 | tf_op jit(solution)/shard_map/dot_general | solution.py:39
  920.1 36.3 %reduce-scatter.2.cloned.1.call-done = f32[64,576]{1,0:T(8,128)} async-done(((f32[512,576]{1,0:T(8,128)}), f32[64,576]{1,0:T(8,128)}) %reduce-scatter.2.cloned.1.call-update) | async-done | bytes 147472 | tf_op jit(solution)/shard_map/reduce_scatter | solution.py:46
  (8 shorter events, 0.0 us)
Async XLA Ops:
  6.5 3.4 copy-start
  6.5 85.9 %all-gather.12.cloned.1.call-start = ((), (), s32[]{:S(2)}) async-start(), calls=%async_computation.4 | async-start | bytes 5242880 | tf_op jit(solution)/shard_map/all_gather | solution.py:26
  7.3 122.1 %all-gather.10.cloned.1.call-start = ((), (), s32[]{:S(2)}) async-start(), calls=%async_computation.3 | async-start | bytes 4718592 | tf_op jit(solution)/shard_map/all_gather | solution.py:22
  8.0 445.6 %all-gather.8.cloned.1.call-start = ((), (), s32[]{:S(2)}) async-start(), calls=%async_computation.2 | async-start | bytes 23592960 | tf_op jit(solution)/shard_map/all_gather | solution.py:20
  8.7 544.0 %all-gather.6.cloned.1.call-start = ((), (), s32[]{:S(2)}) async-start(), calls=%async_computation.1 | async-start | bytes 21233664 | tf_op jit(solution)/shard_map/all_gather | solution.py:25
  9.3 669.0 %all-gather.14.cloned.1.call-start = ((), (), s32[]{:S(2)}) async-start(), calls=%async_computation.5 | async-start | bytes 4718592 | tf_op jit(solution)/shard_map/all_gather | solution.py:23
  9.9 886.5 %all-reduce.2.cloned.1.call-start = ((), (), s32[]{:S(2)}) async-start(), calls=%async_computation.6 | async-start | bytes 8388608 | tf_op jit(solution)/shard_map/psum | solution.py:37
  678.3 218.1 %copy-start.1 = (f32[2048]{0:T(1024)S(1)}, f32[2048]{0:T(1024)}, u32[]{:S(2)}) copy-start(f32[2048]{0:T(1024)} %param.13) | copy-start | bytes 24580
  741.3 215.1 %reduce-scatter.2.cloned.1.call-start = ((), (), s32[]{:S(2)}) async-start(), calls=%async_computation.7 | async-start | bytes 1474560 | tf_op jit(solution)/shard_map/reduce_scatter | solution.py:46
Sparse Core Ops, SparseCore 0:
  8.9 83.4 all-gather.11
  94.3 35.0 all-gather.9
  131.0 322.5 all-gather.7
  455.3 97.4 all-gather.5
  554.5 36.5 all-gather.13
  741.4 154.9 all-reduce.1
  920.2 36.1 reduce-scatter.1
where the time goes:
time: 970 us; the launch traced here: 963 us
  waiting for transfers between devices  665 us (69%)
  matrix products  243 us (25%)
  local copies, waits for them, and re-layouts  40.9 us (4%)
  between operations  13.7 us (1%)
    all_gather x1, waiting for transfers between devices, local(): enc_full = lax.all_gather(enc_tgt, 'row', axis=0, tiled=True)  293 us
    dot_general x2, matrix products, contract_first(): lax.dot_general(left, right, (((0,), (0,)), ((), ())), precision=PRECISE,...  157 us
    psum x1, waiting for transfers between devices, local(): pre_acts = lax.psum(partial_pre, 'row')  155 us
    all_gather x1, waiting for transfers between devices, local(): lax.all_gather(dec_src, 'col', axis=0, tiled=True)  99.2 us
    dot_general x1, matrix products, local(): jnp.dot(eval_full, weighted, precision=PRECISE, preferred_element_type=jn...  62.9 us
    all_gather x1, waiting for transfers between devices, local(): lax.all_gather(tgt_coacts, 'row', axis=0, tiled=True)  41.5 us
    mul x2, local copies, waits for them, and re-layouts, local(): (virtual * coact).reshape(tile_rows, TILE, tile_cols, TILE)  40.9 us
    all_gather x1, waiting for transfers between devices, local(): lax.all_gather(src_coacts, 'col', axis=0, tiled=True)  37 us
  transfers between devices with their start and end apart: 7, of which 6 were waited for; matrix products, arithmetic and copies ran while one was open for 21% of the time, Pallas kernels for 0%

commit v1 on v0

--- a/solution.py
+++ b/solution.py
@@ -34,7 +34,9 @@
         eval_full, weighted, precision=PRECISE, preferred_element_type=jnp.float32
     )
     scale = 1.0 / jnp.sqrt(jnp.float32(S))
-    pre_acts = lax.psum(partial_pre, "row")
+    pre_acts = partial_pre
+    for hop in (1, 2):
+        pre_acts = pre_acts + lax.ppermute(pre_acts, "row", [(dev, dev ^ hop) for dev in range(4)])
     hidden = jnp.maximum(pre_acts * scale + enc_bias[None, :], 0.0)
     recon_part = lax.dot_general(
         hidden,

time: 970 us -> 1100 us (1.13)
  waiting for transfers between devices: 665 us -> 782 us
    ppermute x0 -> x2, waiting for transfers between devices: none -> 271 us  [local(): lax.ppermute(pre_acts, 'row', [(dev, dev ^ hop) for dev in range(4)])]
    psum x1 -> x0, waiting for transfers between devices: 155 us -> none  [local(): pre_acts = lax.psum(partial_pre, 'row')]
  transfers between devices with their start and end apart: 7 -> 8, of which waited for: 6 -> 7; matrix products, arithmetic and copies ran while one was open for 21% -> 19% of each run, Pallas kernels for 0% -> 0%
where the time goes in v1:
time: 1100 us; the launch traced here: 1090 us
  waiting for transfers between devices  782 us (71%)
  matrix products  252 us (23%)
  local copies, waits for them, and re-layouts  40.9 us (4%)
  between operations  13.7 us (1%)
    all_gather x1, waiting for transfers between devices, local(): enc_full = lax.all_gather(enc_tgt, 'row', axis=0, tiled=True)  293 us
    ppermute x2, waiting for transfers between devices, local(): lax.ppermute(pre_acts, 'row', [(dev, dev ^ hop) for dev in range(4)])  271 us
    dot_general x2, matrix products, contract_first(): lax.dot_general(left, right, (((0,), (0,)), ((), ())), precision=PRECISE,...  166 us
    all_gather x1, waiting for transfers between devices, local(): lax.all_gather(dec_src, 'col', axis=0, tiled=True)  99.2 us
    dot_general x1, matrix products, local(): jnp.dot(eval_full, weighted, precision=PRECISE, preferred_element_type=jn...  61.5 us
    all_gather x1, waiting for transfers between devices, local(): lax.all_gather(tgt_coacts, 'row', axis=0, tiled=True)  41.5 us
    mul x2, local copies, waits for them, and re-layouts, local(): (virtual * coact).reshape(tile_rows, TILE, tile_cols, TILE)  40.9 us
    reduce_scatter x1, waiting for transfers between devices, local(): return lax.psum_scatter(recon_part, 'col', scatter_dimension=0, tiled=True)  37.3 us
  transfers between devices with their start and end apart: 8, of which 7 were waited for; matrix products, arithmetic and copies ran while one was open for 19% of the time, Pallas kernels for 0%

profile of v1, /device:TPU:0, one launch (start us, length us, event | category | flops | bytes accessed | tf_op | source)
XLA Modules:
  0.0 1094.2 jit_solution(16324871752322598417)
XLA Ops:
  6.5 0.7 all-gather.12.cloned.1.call-update
  7.3 0.0 all-gather.10.cloned.1.call-start
  7.3 0.7 all-gather.10.cloned.1.call-update
  8.1 0.7 all-gather.8.cloned.1.call-update
  8.8 0.0 all-gather.6.cloned.1.call-start
  8.8 0.5 all-gather.6.cloned.1.call-update
  9.4 0.5 all-gather.14.cloned.1.call-update
  9.9 0.0 reduce-scatter.2.cloned.1.call-start
  10.0 11.9 %mul.29 = f32[32,64,32,64]{3,2,1,0:T(8,128)} broadcast(f32[32,32]{1,0:T(8,128)S(1)} %convert_element_type.3), dimensions={0,2} | broadcast | bytes 16781312 | tf_op jit(solution)/shard_map/mul | solution.py:31
  21.9 28.9 %mul.30 = f32[2048,2048]{1,0:T(8,128)} reshape(f32[32,64,32,64]{3,2,1,0:T(8,128)} %mul.29) | data formatting | bytes 33554432 | tf_op jit(solution)/shard_map/mul | solution.py:31
  50.9 41.5 %all-gather.12.cloned.1.call-done = f32[512,2048]{1,0:T(8,128)} async-done(((f32[128,2048]{1,0:T(8,128)}), f32[512,2048]{1,0:T(8,128)}) %all-gather.12.cloned.1.call-update) | async-done | bytes 4194320 | tf_op jit(solution)/shard_map/all_gather | solution.py:26
  92.4 37.0 %all-gather.10.cloned.1.call-done = f32[512,2048]{1,0:T(8,128)} async-done(((f32[64,2048]{1,0:T(8,128)}), f32[512,2048]{1,0:T(8,128)}) %all-gather.10.cloned.1.call-update) | async-done | bytes 4194320 | tf_op jit(solution)/shard_map/all_gather | solution.py:22
  129.4 31.5 %fusion.20 = f32[2048,2048]{1,0:T(8,128)} fusion(f32[512,2048]{1,0:T(8,128)} %all-gather.10.cloned.1.call-done, f32[512,2048]{1,0:T(8,128)} %all-gather.12.cloned.1.call-done), kind=kOutput, calls=%fused_computation.18 | convolution fusion | flops 25769803776 | bytes 25165824 | tf_op jit(solution)/shard_map/dot_general | solution.py:12
  160.8 292.7 %all-gather.8.cloned.1.call-done = f32[2304,2048]{1,0:T(8,128)} async-done(((f32[576,2048]{1,0:T(8,128)}), f32[2304,2048]{1,0:T(8,128)}) %all-gather.8.cloned.1.call-update) | async-done | bytes 18874384 | tf_op jit(solution)/shard_map/all_gather | solution.py:20
  453.6 99.2 %all-gather.6.cloned.1.call-done = f32[2304,2048]{1,0:T(8,128)} async-done(((f32[288,2048]{1,0:T(8,128)}), f32[2304,2048]{1,0:T(8,128)}) %all-gather.6.cloned.1.call-update) | async-done | bytes 18874384 | tf_op jit(solution)/shard_map/all_gather | solution.py:25
  552.8 134.8 %fusion.19 = f32[2048,2048]{1,0:T(8,128)} fusion(f32[2304,2048]{1,0:T(8,128)} %all-gather.6.cloned.1.call-done, f32[2304,2048]{1,0:T(8,128)} %all-gather.8.cloned.1.call-done), kind=kOutput, calls=%fused_computation.17 | convolution fusion | flops 115964116992 | bytes 54525952 | tf_op jit(solution)/shard_map/dot_general | solution.py:12
  687.6 61.5 %fusion.10 = f32[512,2048]{0,1:T(8,128)S(1)} fusion(f32[512,2048]{1,0:T(8,128)} %all-gather.14.cloned.1.call-done, f32[2048,2048]{1,0:T(8,128)} %mul.30, f32[2048,2048]{1,0:T(8,128)} %fusion.19, f32[2048,2048]{1,0:T(8,128)} %fusion.20), kind=kOutput, calls=%fused_computation.10 | convolution fusion | flops 25782386688 | bytes 58720256 | tf_op jit(solution)/shard_map/dot_general | solution.py:33
  749.1 1.6 collective-permute-start
  750.7 91.2 %collective-permute-done = f32[512,2048]{0,1:T(8,128)S(1)} collective-permute-done((f32[512,2048]{0,1:T(8,128)S(1)}, f32[512,2048]{0,1:T(8,128)S(1)}, u32[]{:S(2)}, u32[]{:S(2)}) %collective-permute-start) | collective-permute-done | bytes 4194336 | tf_op jit(solution)/shard_map/ppermute | solution.py:39
  841.9 1.0 add.16
  843.0 2.5 collective-permute-start.1
  845.4 180.2 %collective-permute-done.1 = f32[512,2048]{0,1:T(8,128)S(1)} collective-permute-done((f32[512,2048]{0,1:T(8,128)S(1)}, f32[512,2048]{0,1:T(8,128)S(1)}, u32[]{:S(2)}, u32[]{:S(2)}) %collective-permute-start.1) | collective-permute-done | bytes 4194336 | tf_op jit(solution)/shard_map/ppermute | solution.py:39
  1025.7 24.2 %fusion.5 = f32[512,576]{1,0:T(8,128)} fusion(f32[576,2048]{1,0:T(8,128)} %param.14, f32[512,2048]{0,1:T(8,128)S(1)} %add.16, f32[512,2048]{0,1:T(8,128)S(1)} %collective-permute-done.1, f32[2048]{0:T(1024)S(1)} %copy-done.1), kind=kOutput, calls=%fused_computation.5 | convolution fusion | flops 7251951616 | bytes 14295040 | tf_op jit(solution)/shard_map/dot_general | solution.py:41
  1049.9 37.3 %reduce-scatter.2.cloned.1.call-done = f32[64,576]{1,0:T(8,128)} async-done(((f32[512,576]{1,0:T(8,128)}), f32[64,576]{1,0:T(8,128)}) %reduce-scatter.2.cloned.1.call-update) | async-done | bytes 147472 | tf_op jit(solution)/shard_map/reduce_scatter | solution.py:48
  (10 shorter events, 0.1 us)
Async XLA Ops:
  6.5 85.9 %all-gather.12.cloned.1.call-start = ((), (), s32[]{:S(2)}) async-start(), calls=%async_computation.4 | async-start | bytes 5242880 | tf_op jit(solution)/shard_map/all_gather | solution.py:26
  7.3 2.7 copy-start
  7.3 122.1 %all-gather.10.cloned.1.call-start = ((), (), s32[]{:S(2)}) async-start(), calls=%async_computation.3 | async-start | bytes 4718592 | tf_op jit(solution)/shard_map/all_gather | solution.py:22
  8.0 445.6 %all-gather.8.cloned.1.call-start = ((), (), s32[]{:S(2)}) async-start(), calls=%async_computation.2 | async-start | bytes 23592960 | tf_op jit(solution)/shard_map/all_gather | solution.py:20
  8.8 544.0 %all-gather.6.cloned.1.call-start = ((), (), s32[]{:S(2)}) async-start(), calls=%async_computation.1 | async-start | bytes 21233664 | tf_op jit(solution)/shard_map/all_gather | solution.py:25
  9.3 678.3 %all-gather.14.cloned.1.call-start = ((), (), s32[]{:S(2)}) async-start(), calls=%async_computation.5 | async-start | bytes 4718592 | tf_op jit(solution)/shard_map/all_gather | solution.py:23
  9.9 1077.3 %reduce-scatter.2.cloned.1.call-start = ((), (), s32[]{:S(2)}) async-start(), calls=%async_computation.6 | async-start | bytes 1474560 | tf_op jit(solution)/shard_map/reduce_scatter | solution.py:48
  749.1 276.5 %copy-start.1 = (f32[2048]{0:T(1024)S(1)}, f32[2048]{0:T(1024)}, u32[]{:S(2)}) copy-start(f32[2048]{0:T(1024)} %param.13) | copy-start | bytes 24580
  749.1 92.8 %collective-permute-start = (f32[512,2048]{0,1:T(8,128)S(1)}, f32[512,2048]{0,1:T(8,128)S(1)}, u32[]{:S(2)}, u32[]{:S(2)}) collective-permute-start(f32[512,2048]{0,1:T(8,128)S(1)} %fusion.10), channel_id=1, source_target_pairs={{0,8},{8,0},{16,24},{24,16},{1,9},{9,1},{17,25},{25,17},{2,10},{10... | collective-permute-start | bytes 12582920 | tf_op jit(solution)/shard_map/ppermute | solution.py:39
  843.0 182.7 %collective-permute-start.1 = (f32[512,2048]{0,1:T(8,128)S(1)}, f32[512,2048]{0,1:T(8,128)S(1)}, u32[]{:S(2)}, u32[]{:S(2)}) collective-permute-start(f32[512,2048]{0,1:T(8,128)S(1)} %add.16), channel_id=1, source_target_pairs={{0,16},{8,24},{16,0},{24,8},{1,17},{9,25},{17,1},{25,9},{2,18},{10... | collective-permute-start | bytes 12582920 | tf_op jit(solution)/shard_map/ppermute | solution.py:39
Sparse Core Ops, SparseCore 0:
  8.9 83.4 all-gather.11
  94.3 35.0 all-gather.9
  131.0 322.5 all-gather.7
  455.3 97.4 all-gather.5
  554.5 36.5 all-gather.13
  1050.0 37.1 reduce-scatter.1
